TPU v7x, 32 devices: a whole 2x2x4 slice. The times are simulated.
32 devices in a mesh: line: 16 (over z, y, x), sec: 2 (over core).
Axes of the slice: x: 2, y: 2, z: 4, core: 2. Of those that a mesh axis runs over, the one named last changes fastest.
Arguments:
- right_side: float32 [16, 2, 256, 256], P('line', 'sec'), may hold values from -80 to 80
- inverse_diag: float32 [16, 2, 256, 256], P('line', 'sec'), may hold values from -3 to 3
- couplings: float32 [16, 2, 2, 256, 256], P('line', 'sec'), may hold values from -0.5 to 0.5
- neighbors: int32 [16, 2, 2], P('line', 'sec'), may hold values from -1 to 0, as said below
Outputs:
- panel: float32 [16, 2, 256, 256], P('line', 'sec')
- factor: float32 [256, 256], replicated
Inputs may be any that keep to these rules, and one draw needn't show every extreme that they name: `neighbors`: every entry is -1 or a section lower than its own; slot 0 of every section after the first names the section just before it; the first section's entries are all -1.
All inputs are finite; a program needn't handle non-finite values.
Results may differ from a plain program's by a relative error of at most 0.0001.
Values sent between devices are 32-bit elements; how exact they have to be, the bound alone decides.
No kernel may reach another device: no remote copies, remote signals or barrier semaphores. Data moves between devices by JAX's collectives and lax.ppermute only.
A program may use at most 64 MiB of HBM per device.

v0:
```python
import jax
import jax.numpy as jnp
from jax import lax
from jax.sharding import PartitionSpec as P


def broadcast(array, axis, root):
    mine = lax.axis_index(axis) == root
    return lax.psum(jnp.where(mine, array, jnp.zeros_like(array)), axis)


def exact_dot(left, right):
    return jnp.dot(left, right, precision=lax.Precision.HIGHEST, preferred_element_type=jnp.float32)


def solve_here(acc, inverse, mine):
    return lax.cond(
        mine, lambda value: exact_dot(inverse, value), lambda value: jnp.zeros_like(value), acc
    )


def absorb(acc, coupled, links, anchor, arrived):
    for slot in range(coupled.shape[0]):
        matrix = coupled[slot]
        acc = lax.cond(
            links[slot] == anchor,
            lambda value, mat=matrix: value - exact_dot(mat, arrived),
            lambda value: value,
            acc,
        )
    return acc


def gram_sum(matrix):
    local = exact_dot(matrix.T, matrix)
    return lax.psum(local, ("line", "sec"))


def upper_factor(matrix, total):
    lower = jnp.linalg.cholesky(gram_sum(matrix) / total)
    normed = jax.scipy.linalg.solve_triangular(lower, matrix.T, lower=True).T
    return (normed, lower.T)


def shards(right_side, inverse_diag, couplings, neighbors):
    target = right_side[0, 0]
    inverse = inverse_diag[0, 0]
    coupled = couplings[0, 0]
    links = neighbors[0, 0]
    section = lax.axis_index("sec")
    count = lax.axis_size("sec")
    acc = target
    solved = jnp.zeros_like(target)
    for anchor in range(count):
        mine = section == anchor
        candidate = solve_here(acc, inverse, mine)
        arrived = broadcast(candidate, "sec", anchor)
        solved = jnp.where(mine, arrived, solved)
        acc = absorb(acc, coupled, links, anchor, arrived)
    total = jnp.float32(lax.axis_size("line") * count * target.shape[0])
    second, factor = upper_factor(solved, total)
    return (second[None, None], factor)


def solution(mesh):
    placed = (
        P("line", "sec", None, None),
        P("line", "sec", None, None),
        P("line", "sec", None, None, None),
        P("line", "sec", None),
    )
    return jax.shard_map(
        shards,
        mesh=mesh,
        in_specs=placed,
        out_specs=(P("line", "sec", None, None), P()),
        check_vma=False,
    )
```

profile of v0, /device:TPU:0, one launch (start us, length us, event | category | flops | bytes accessed | tf_op | source)
XLA Modules:
  0.0 260.2 jit_solution(11902350834891242868)
XLA Ops:
  7.2 0.0 copy-start.1
  7.2 0.0 all-reduce.5.cloned.1.call-start
  7.2 1.0 copy.33
  8.2 0.0 copy-done.1
  8.2 0.4 conditional.4
  8.2 0.4 fusion.19
  8.6 0.0 copy-start.4
  8.6 0.7 broadcast_select_fusion.1
  9.3 0.0 all-reduce.5.cloned.1.call-update
  9.4 0.0 all-reduce.7.cloned.1.call-start
  9.4 0.0 copy-start.5
  9.4 0.6 copy-done.5
  10.1 0.6 fusion.18
  11.9 20.0 %all-reduce.5.cloned.1.call-done = f32[256,256]{1,0:T(8,128)} async-done(((f32[256,256]{1,0:T(8,128)}), f32[256,256]{1,0:T(8,128)}) %all-reduce.5.cloned.1.call-update) | async-done | bytes 262160 | tf_op jit(solution)/shard_map/psum | solution.py:9
  31.9 0.0 copy-done.4
  31.9 0.7 broadcast_select_fusion
  32.6 0.0 copy-start
  32.6 0.0 all-reduce.7.cloned.1.call-update
  32.6 0.0 all-reduce.9.cloned.1.call-start
  32.7 22.7 %all-reduce.7.cloned.1.call-done = f32[256,256]{1,0:T(8,128)} async-done(((f32[256,256]{1,0:T(8,128)}), f32[256,256]{1,0:T(8,128)}) %all-reduce.7.cloned.1.call-update) | async-done | bytes 262160 | tf_op jit(solution)/shard_map/psum | solution.py:9
  55.4 0.0 copy-done
  55.4 1.3 fusion.10
  56.7 0.0 copy-start.3
  56.7 0.0 all-reduce.9.cloned.1.call-update
  56.7 0.9 copy-done.3
  57.7 131.5 %all-reduce.9.cloned.1.call-done = f32[256,256]{0,1:T(8,128)} async-done(((f32[256,256]{0,1:T(8,128)}), f32[256,256]{0,1:T(8,128)}) %all-reduce.9.cloned.1.call-update) | async-done | bytes 262160 | tf_op jit(solution)/shard_map/psum | solution.py:36
  189.2 1.0 broadcast_multiply_fusion
  190.2 0.0 copy-start.2
  190.2 0.1 copy.7
  190.3 0.8 copy-done.2
  191.2 11.7 %cholesky.49 = f32[128,128]{1,0:T(8,128)S(1)} custom-call(f32[128,128]{1,0:T(8,128)S(1)} %cholesky.115), custom_call_target="Cholesky" | custom-call | tf_op jit(solution)/shard_map/jit(cholesky)/cholesky | solution.py:40
  203.0 9.8 %custom-call.15 = f32[1,128,128]{1,2,0:T(8,128)S(1)} custom-call(f32[1,128,128]{2,1,0:T(8,128)S(1)} %get-tuple-element.75), custom_call_target="InvertDiagBlocksLowerTriangular" | custom-call | tf_op jit(solution)/shard_map/jit(cholesky)/cholesky | solution.py:40
  212.8 0.2 constant_dynamic-update-slice_fusion.1
  213.0 0.3 convolution_subtract_fusion.3
  213.3 11.7 %cholesky.103 = f32[128,128]{1,0:T(8,128)S(1)} custom-call(f32[128,128]{1,0:T(8,128)S(1)} %convolution_subtract_fusion.3), custom_call_target="Cholesky" | custom-call | tf_op jit(solution)/shard_map/jit(cholesky)/cholesky | solution.py:40
  225.0 0.6 compare_reduce_fusion
  227.0 0.1 triangular_solve.57
  227.1 4.1 %while.1 = (s32[]{:T(128)}, f32[256,256]{1,0:T(8,128)S(1)}, s32[2,2]{1,0:T(2,128)S(1)}, f32[2,128,128]{2,1,0:T(8,128)S(1)}, s32[]{:T(128)}) while((s32[]{:T(128)}, f32[256,256]{1,0:T(8,128)S(1)}, s32[2,2]{1,0:T(2,128)S(1)}, f32[2,128,128]{2,1,0:T(8,128)S(1)}, s32[]{:T(128)}) %tuple.60), condition=%wide.while_cond, body=%wide.while_body.sunk | while | flops 2 | bytes 131189 | solution.py:41
  227.2 0.6 fusion.32
  227.8 1.4 bitcast_dynamic-update-slice_fusion.2
  229.2 0.6 fusion.32
  229.8 1.4 bitcast_dynamic-update-slice_fusion.2
  231.2 19.7 %custom-call.16 = f32[2,128,128]{1,2,0:T(8,128)S(1)} custom-call(f32[2,128,128]{2,1,0:T(8,128)S(1)} %get-tuple-element.57), custom_call_target="InvertDiagBlocksLowerTriangular" | custom-call | tf_op jit(solution)/shard_map/jit(_solve_triangular)/triangular_solve | solution.py:41
  250.9 0.3 fusion.7
  251.2 0.4 convolution_subtract_fusion.2
  251.6 0.3 fusion.12
  252.0 0.8 copy.8
  252.8 0.8 copy.9
  (16 shorter events, 0.3 us)
Async XLA Ops:
  7.2 1.0 copy-start.1
  7.2 24.7 %all-reduce.5.cloned.1.call-start = ((), (), s32[]{:S(2)}) async-start(), calls=%async_computation | async-start | bytes 524288 | tf_op jit(solution)/shard_map/psum | solution.py:9
  8.6 23.3 %copy-start.4 = (f32[1,1,2,256,256]{4,3,2,1,0:T(8,128)S(1)}, f32[1,1,2,256,256]{4,3,2,1,0:T(8,128)}, u32[]{:S(2)}) copy-start(f32[1,1,2,256,256]{4,3,2,1,0:T(8,128)} %param.14) | copy-start | bytes 1572868
  9.4 46.0 %all-reduce.7.cloned.1.call-start = ((), (), s32[]{:S(2)}) async-start(), calls=%async_computation.1 | async-start | bytes 524288 | tf_op jit(solution)/shard_map/psum | solution.py:9
  9.4 0.7 copy-start.5
  32.6 22.8 %copy-start = (f32[256,256]{1,0:T(8,128)S(1)}, f32[256,256]{1,0:T(8,128)}, u32[]{:S(2)}) copy-start(f32[256,256]{1,0:T(8,128)} %all-reduce.5.cloned.1.call-done) | copy-start | bytes 786436
  32.6 156.6 %all-reduce.9.cloned.1.call-start = ((), (), s32[]{:S(2)}) async-start(), calls=%async_computation.2 | async-start | bytes 524288 | tf_op jit(solution)/shard_map/psum | solution.py:36
  56.7 0.9 copy-start.3
  190.2 1.0 copy-start.2
Sparse Core Ops, SparseCore 0:
  10.9 20.9 all-reduce.4
  34.8 20.5 all-reduce.6
  61.5 127.7 all-reduce.8
where the time goes:
time: 261 us; the launch traced here: 260 us
  waiting for transfers between devices  174 us (67%)
  other arithmetic  56.2 us (22%)
  between operations  16.5 us (6%)
  local copies, waits for them, and re-layouts  9.83 us (4%)
  matrix products  3.18 us (1%)
    psum x1, waiting for transfers between devices, gram_sum(): return lax.psum(local, ('line', 'sec'))  132 us
    psum x2, waiting for transfers between devices, broadcast(): return lax.psum(jnp.where(mine, array, jnp.zeros_like(array)), axis)  42.6 us
    another operation x6, other arithmetic, upper_factor(): lower = jnp.linalg.cholesky(gram_sum(matrix) / total)  33.9 us
    another operation x2, other arithmetic, upper_factor(): normed = jax.scipy.linalg.solve_triangular(lower, matrix.T, lower=True).T  19.7 us
  transfers between devices with their start and end apart: 3, of which 3 were waited for; matrix products, arithmetic and copies ran while one was open for 0% of the time, Pallas kernels for 0%

commit v1 on v0

--- a/solution.py
+++ b/solution.py
@@ -6,7 +6,7 @@
 
 def broadcast(array, axis, root):
     mine = lax.axis_index(axis) == root
-    return lax.psum(jnp.where(mine, array, jnp.zeros_like(array)), axis)
+    return jnp.sum(lax.all_gather(jnp.where(mine, array, jnp.zeros_like(array)), axis), axis=0)
 
 
 def exact_dot(left, right):

time: 261 us -> 220 us (0.84)
  waiting for transfers between devices: 174 us -> 130 us
  blocking collectives: 0 us -> 5 us
    psum x2 -> x0, waiting for transfers between devices: 42.6 us -> none  [broadcast(): return lax.psum(jnp.where(mine, array, jnp.zeros_like(array)), axis)]
    all_gather x0 -> x2, blocking collectives: none -> 5 us  [broadcast(): lax.all_gather(jnp.where(mine, array, jnp.zeros_like(array)), axis)]
  transfers between devices with their start and end apart: 3 -> 1, of which waited for: 3 -> 1; matrix products, arithmetic and copies ran while one was open for 0% -> 0% of each run, Pallas kernels for 0% -> 0%
where the time goes in v1:
time: 220 us
  waiting for transfers between devices  130 us (59%)
  other arithmetic  54.8 us (25%)
  between operations  16.8 us (8%)
  local copies, waits for them, and re-layouts  9.97 us (5%)
  blocking collectives  5 us (2%)
  matrix products  3.17 us (1%)
    psum x1, waiting for transfers between devices, gram_sum(): return lax.psum(local, ('line', 'sec'))  130 us
    another operation x6, other arithmetic, upper_factor(): lower = jnp.linalg.cholesky(gram_sum(matrix) / total)  33.9 us
    another operation x2, other arithmetic, upper_factor(): normed = jax.scipy.linalg.solve_triangular(lower, matrix.T, lower=True).T  19.7 us
    unnamed x11, local copies, waits for them, and re-layouts  5.13 us
    all_gather x2, blocking collectives, broadcast(): lax.all_gather(jnp.where(mine, array, jnp.zeros_like(array)), axis)  5 us
  transfers between devices with their start and end apart: 1, of which 1 were waited for; matrix products, arithmetic and copies ran while one was open for 0% of the time, Pallas kernels for 0%

profile of v1, /device:TPU:0, one launch (start us, length us, event | category | flops | bytes accessed | tf_op | source)
XLA Modules:
  0.0 219.9 jit_solution(6540483129204124155)
XLA Ops:
  7.2 0.0 copy-start
  7.2 0.0 all-reduce.3.cloned.1.call-start
  7.2 1.0 copy.31
  8.2 0.0 copy-start.3
  8.2 0.7 copy-done.3
  8.9 0.6 fusion.18
  10.8 0.0 copy-done
  10.8 0.4 conditional.4
  10.8 0.4 fusion.19
  11.2 2.2 all-gather
  13.4 0.0 copy-start.2
  13.5 1.0 copy-done.2
  14.5 2.8 %all-gather.1 = f32[512,256]{1,0:T(8,128)S(1)} all-gather(f32[256,256]{1,0:T(8,128)S(1)} %broadcast_select_fusion), channel_id=3, replica_groups=mesh['line'=16,'sec'=2] {'sec'}, dimensions={0}, use_global_device_ids=true | all-gather | bytes 786432 | tf_op jit(solution)/shard_map/all_gather | solution.py:9
  17.4 1.3 fusion.10
  18.7 0.0 all-reduce.3.cloned.1.call-update
  18.8 129.8 %all-reduce.3.cloned.1.call-done = f32[256,256]{0,1:T(8,128)} async-done(((f32[256,256]{0,1:T(8,128)}), f32[256,256]{0,1:T(8,128)}) %all-reduce.3.cloned.1.call-update) | async-done | bytes 262160 | tf_op jit(solution)/shard_map/psum | solution.py:36
  148.6 1.0 broadcast_multiply_fusion
  149.6 0.0 copy-start.1
  149.6 0.1 copy.7
  149.7 0.8 copy-done.1
  150.6 11.7 %cholesky.49 = f32[128,128]{1,0:T(8,128)S(1)} custom-call(f32[128,128]{1,0:T(8,128)S(1)} %cholesky.115), custom_call_target="Cholesky" | custom-call | tf_op jit(solution)/shard_map/jit(cholesky)/cholesky | solution.py:40
  162.4 9.8 %custom-call.15 = f32[1,128,128]{1,2,0:T(8,128)S(1)} custom-call(f32[1,128,128]{2,1,0:T(8,128)S(1)} %get-tuple-element.75), custom_call_target="InvertDiagBlocksLowerTriangular" | custom-call | tf_op jit(solution)/shard_map/jit(cholesky)/cholesky | solution.py:40
  172.2 0.2 constant_dynamic-update-slice_fusion.1
  172.4 0.3 convolution_subtract_fusion.3
  172.7 11.7 %cholesky.103 = f32[128,128]{1,0:T(8,128)S(1)} custom-call(f32[128,128]{1,0:T(8,128)S(1)} %convolution_subtract_fusion.3), custom_call_target="Cholesky" | custom-call | tf_op jit(solution)/shard_map/jit(cholesky)/cholesky | solution.py:40
  184.4 0.6 compare_reduce_fusion
  186.4 0.1 triangular_solve.57
  186.5 4.1 %while.1 = (s32[]{:T(128)}, f32[256,256]{1,0:T(8,128)S(1)}, s32[2,2]{1,0:T(2,128)S(1)}, f32[2,128,128]{2,1,0:T(8,128)S(1)}, s32[]{:T(128)}) while((s32[]{:T(128)}, f32[256,256]{1,0:T(8,128)S(1)}, s32[2,2]{1,0:T(2,128)S(1)}, f32[2,128,128]{2,1,0:T(8,128)S(1)}, s32[]{:T(128)}) %tuple.60), condition=%wide.while_cond, body=%wide.while_body.sunk | while | flops 2 | bytes 131189 | solution.py:41
  186.6 0.6 fusion.32
  187.2 1.4 bitcast_dynamic-update-slice_fusion.2
  188.6 0.6 fusion.32
  189.2 1.4 bitcast_dynamic-update-slice_fusion.2
  190.6 19.7 %custom-call.16 = f32[2,128,128]{1,2,0:T(8,128)S(1)} custom-call(f32[2,128,128]{2,1,0:T(8,128)S(1)} %get-tuple-element.57), custom_call_target="InvertDiagBlocksLowerTriangular" | custom-call | tf_op jit(solution)/shard_map/jit(_solve_triangular)/triangular_solve | solution.py:41
  210.3 0.3 fusion.7
  210.6 0.4 convolution_subtract_fusion.2
  211.0 0.3 fusion.12
  211.4 0.8 copy.8
  212.2 0.8 copy.9
  (20 shorter events, 0.4 us)
Async XLA Ops:
  7.2 3.6 %copy-start = (f32[1,1,256,256]{3,2,1,0:T(8,128)S(1)}, f32[1,1,256,256]{3,2,1,0:T(8,128)}, u32[]{:S(2)}) copy-start(f32[1,1,256,256]{3,2,1,0:T(8,128)} %param.13) | copy-start | bytes 786436
  7.2 141.5 %all-reduce.3.cloned.1.call-start = ((), (), s32[]{:S(2)}) async-start(), calls=%async_computation | async-start | bytes 524288 | tf_op jit(solution)/shard_map/psum | solution.py:36
  8.2 0.7 copy-start.3
  13.4 1.0 copy-start.2
  149.6 1.0 copy-start.1
Sparse Core Ops, SparseCore 0:
  18.8 129.7 all-reduce.2
